TPU v7x, 512 devices: a whole 4x8x8 slice. The times are simulated.
512 devices in a mesh: ta: 64 (over z, x, core), pa: 8 (over y).
Axes of the slice: x: 4, y: 8, z: 8, core: 2. Of those that a mesh axis runs over, the one named last changes fastest.
Arguments:
- occupied_orbitals: bfloat16 [4096, 512], P('pa'), may hold values from -3 to 3
- virtual_orbitals: bfloat16 [4096, 1536], P('pa'), may hold values from -2.5 to 2.5
- occupied_gaps: float32 [512], replicated, may hold values from 0.05 to 2
- virtual_gaps: float32 [1536], replicated, may hold values from 0.05 to 2
- tile_columns: int32 [32, 8], replicated, may hold values from 0 to 31, as said below
- probe_vectors: bfloat16 [32, 4096], P(None, 'ta'), may hold values from -0.1875 to 0.1875
Outputs:
- response: float32 [64, 32, 4096], P('ta', None, 'pa')
Inputs may be any that keep to these rules, and one draw needn't show every extreme that they name: `tile_columns`: each row block lists 8 different column blocks, and every column block is listed by some row block.
All inputs are finite; a program needn't handle non-finite values.
Results may differ from a plain program's by a relative error of at most 0.00083.
Values may be sent and summed in bfloat16 or wider, within the bound.
A program may use at most 64 MiB of HBM per device.

v0:
```python
import jax
import jax.numpy as jnp
from jax import lax
from jax.sharding import PartitionSpec as P

BLK = 128
NT = 32
NVEC = 32
F_DEV = 1


def spread(value, axis, source):
    kept = jnp.where(lax.axis_index(axis) == source, value, 0).astype(value.dtype)
    return lax.psum(kept, axis)


def quadrature_grids(count_times, count_freqs):
    low_time = jnp.log(jnp.float32(0.05))
    high_time = jnp.log(jnp.float32(8.0))
    time_place = (jnp.arange(count_times, dtype=jnp.float32) + 0.5) / count_times
    times_grid = jnp.exp(low_time + (high_time - low_time) * time_place)
    weights_grid = times_grid * (high_time - low_time) / count_times
    low_freq = jnp.log(jnp.float32(0.05))
    high_freq = jnp.log(jnp.float32(20.0))
    freq_place = (jnp.arange(count_freqs, dtype=jnp.float32) + 0.5) / count_freqs
    freqs_grid = jnp.exp(low_freq + (high_freq - low_freq) * freq_place)
    cosine_table = 2.0 * weights_grid[None, :] * jnp.cos(freqs_grid[:, None] * times_grid[None, :])
    return (times_grid, cosine_table)


def shards(
    occupied_orbitals, virtual_orbitals, occupied_gaps, virtual_gaps, tile_columns, probe_vectors
):
    count_ta = lax.axis_size("ta")
    panel_rows = occupied_orbitals.shape[0]
    slice_width = probe_vectors.shape[1]
    occ_count = occupied_orbitals.shape[1]
    block_count = panel_rows // BLK
    first_block = lax.axis_index("pa") * block_count
    times_grid, cosine_table = quadrature_grids(NT, F_DEV * count_ta)
    occ_weights = jnp.exp(-times_grid[:, None] * occupied_gaps[None, :])
    virt_weights = jnp.exp(-times_grid[:, None] * virtual_gaps[None, :])
    start_terms = jnp.zeros((NT, NVEC, panel_rows), jnp.float32)
    slice_start = lax.axis_index("ta") * slice_width
    owner_panel = slice_start // panel_rows
    offset_rows = slice_start % panel_rows
    local_part = jnp.concatenate(
        [
            lax.dynamic_slice_in_dim(occupied_orbitals, offset_rows, slice_width, 0),
            lax.dynamic_slice_in_dim(virtual_orbitals, offset_rows, slice_width, 0),
        ],
        axis=1,
    )
    column_part = spread(local_part, "pa", owner_panel)
    column_occ = column_part[:, :occ_count]
    column_virt = column_part[:, occ_count:]
    scaled_occ = (column_occ[None].astype(jnp.float32) * occ_weights[:, None, :]).astype(
        jnp.bfloat16
    )
    scaled_virt = (column_virt[None].astype(jnp.float32) * virt_weights[:, None, :]).astype(
        jnp.bfloat16
    )
    panel_tiles = lax.dynamic_slice_in_dim(tile_columns, first_block, block_count, 0)
    column_blocks = (slice_start + jnp.arange(slice_width, dtype=jnp.int32)) // BLK
    present = jnp.any(panel_tiles[:, :, None] == column_blocks[None, None, :], axis=1)
    column_mask = present.astype(jnp.float32)
    empty_terms = jnp.zeros((NT, NVEC, BLK), jnp.float32)

    def block_result(which_block):
        row_occ = lax.dynamic_slice_in_dim(occupied_orbitals, which_block * BLK, BLK, 0)
        row_virt = lax.dynamic_slice_in_dim(virtual_orbitals, which_block * BLK, BLK, 0)
        green_occ = jnp.einsum(
            "tci,ri->tcr", scaled_occ, row_occ, preferred_element_type=jnp.float32
        )
        green_virt = jnp.einsum(
            "tca,ra->tcr", scaled_virt, row_virt, preferred_element_type=jnp.float32
        )
        mask_row = column_mask[which_block]
        polar = (green_occ * green_virt * mask_row[None, :, None]).astype(jnp.bfloat16)
        return jnp.einsum("vc,tcr->tvr", probe_vectors, polar, preferred_element_type=jnp.float32)

    def visit_block(time_terms, which_block):
        block_terms = lax.cond(
            jnp.any(present[which_block]),
            block_result,
            lambda skipped_block: empty_terms,
            which_block,
        )
        return (
            lax.dynamic_update_slice_in_dim(time_terms, block_terms, which_block * BLK, 2),
            None,
        )

    time_terms, _ = lax.scan(visit_block, start_terms, jnp.arange(block_count, dtype=jnp.int32))
    highest = lax.Precision.HIGHEST
    partial_response = jnp.einsum("kt,tvr->kvr", cosine_table, time_terms, precision=highest)
    response = lax.psum_scatter(partial_response, "ta", scatter_dimension=0, tiled=True)
    return response


def solution(mesh):
    placed = (P("pa", None), P("pa", None), P(), P(), P(), P(None, "ta"))
    return jax.shard_map(
        shards, mesh=mesh, in_specs=placed, out_specs=P("ta", None, "pa"), check_vma=False
    )
```

profile of v0, /device:TPU:8, one launch (start us, length us, event | category | flops | bytes accessed | tf_op | source)
XLA Modules:
  0.0 357.0 jit_solution(4372442676124110581)
XLA Ops:
  10.6 1.5 multiply_exponential_fusion
  13.2 1.4 multiply_exponential_fusion.1
  14.6 77.7 %all-reduce.3.cloned.1.call-done = bf16[64,2048]{1,0:T(8,128)(2,1)} async-done(((bf16[64,2048]{1,0:T(8,128)(2,1)}), bf16[64,2048]{1,0:T(8,128)(2,1)}) %all-reduce.3.cloned.1.call-update) | async-done | bytes 262160 | tf_op jit(solution)/shard_map/psum | solution.py:14
  93.3 1.5 slice_convert_fusion.1
  95.3 1.6 broadcast_in_dim.7.clone
  96.9 56.1 %while.11 = (s32[]{:T(128)}, f32[32,32,512]{2,0,1:T(8,128)}, s32[4]{0:T(128)}, pred[4,64]{1,0:T(4,128)(4,1)}, bf16[512,512]{1,0:T(8,128)(2,1)}, /*index=5*/bf16[...) while((s32[]{:T(128)}, f32[32,32,512]{2,0,1:T(8,128)}, ...), condition=%wide.region_6.7_spmd.clone, body=%wide.region_2.6_spmd.clone.sunk | while | flops 1099694208 | bytes 21763300 | solution.py:94
  96.9 1.3 dynamic_slice.49
  100.2 1.3 dynamic-slice_reduce_fusion.2
  102.1 5.4 %multiply_convert_fusion.5 = bf16[32,64,1536]{2,1,0:T(8,128)(2,1)} fusion(f32[32,1536]{1,0:T(8,128)} %get-tuple-element.256, f32[64,1536]{1,0:T(8,128)S(1)} %get-tuple-element.257), kind=kLoop, calls=%fused_computation.19.clone.1 | loop fusion | flops 6291456 | bytes 6881280 | tf_op jit(solution)/shard_map/convert_element_type | solution.py:60
  107.5 1.5 multiply_convert_fusion.4
  110.9 1.3 dynamic_slice.49
  114.3 1.3 dynamic-slice_reduce_fusion.2
  116.1 5.4 %multiply_convert_fusion.5 = bf16[32,64,1536]{2,1,0:T(8,128)(2,1)} fusion(f32[32,1536]{1,0:T(8,128)} %get-tuple-element.256, f32[64,1536]{1,0:T(8,128)S(1)} %get-tuple-element.257), kind=kLoop, calls=%fused_computation.19.clone.1 | loop fusion | flops 6291456 | bytes 6881280 | tf_op jit(solution)/shard_map/convert_element_type | solution.py:60
  121.5 1.5 multiply_convert_fusion.4
  125.0 1.3 dynamic_slice.49
  128.3 1.3 dynamic-slice_reduce_fusion.2
  130.1 5.4 %multiply_convert_fusion.5 = bf16[32,64,1536]{2,1,0:T(8,128)(2,1)} fusion(f32[32,1536]{1,0:T(8,128)} %get-tuple-element.256, f32[64,1536]{1,0:T(8,128)S(1)} %get-tuple-element.257), kind=kLoop, calls=%fused_computation.19.clone.1 | loop fusion | flops 6291456 | bytes 6881280 | tf_op jit(solution)/shard_map/convert_element_type | solution.py:60
  135.5 1.5 multiply_convert_fusion.4
  139.0 1.3 dynamic_slice.49
  144.2 5.4 %multiply_convert_fusion.5 = bf16[32,64,1536]{2,1,0:T(8,128)(2,1)} fusion(f32[32,1536]{1,0:T(8,128)} %get-tuple-element.256, f32[64,1536]{1,0:T(8,128)S(1)} %get-tuple-element.257), kind=kLoop, calls=%fused_computation.19.clone.1 | loop fusion | flops 6291456 | bytes 6881280 | tf_op jit(solution)/shard_map/convert_element_type | solution.py:60
  149.5 1.5 multiply_convert_fusion.4
  153.0 5.3 %fusion.22 = f32[64,32,512]{2,0,1:T(8,128)S(1)} fusion(f32[32,32,512]{2,0,1:T(8,128)} %get-tuple-element.81, f32[32]{0:T(128)} %get-tuple-element.137, f32[64]{0:T(128)} %add_exponential_fusion, f32[32]{0:T(128)} %get-tuple-element.138), kind=kOutput, calls=%fused_computation.28 | convolution fusion | flops 402657280 | bytes 6291968 | tf_op jit(solution)/shard_map/kt,tvr->kvr/dot_general | solution.py:96
  158.4 4.4 %copy.15 = f32[64,32,512]{2,1,0:T(8,128)} copy(f32[64,32,512]{2,0,1:T(8,128)S(1)} %fusion.22) | data formatting | bytes 8388608 | tf_op jit(solution)/shard_map/kt,tvr->kvr/dot_general | solution.py:96
  162.8 187.4 %reduce-scatter.4.cloned.1.call-done = f32[1,32,512]{2,1,0:T(8,128)} async-done(((f32[64,32,512]{2,1,0:T(8,128)}), f32[1,32,512]{2,1,0:T(8,128)}) %reduce-scatter.4.cloned.1.call-update) | async-done | bytes 65552
  (34 shorter events, 13.0 us)
Async XLA Ops:
  6.5 3.3 copy-start
  6.5 85.8 %all-reduce.3.cloned.1.call-start = ((), (), s32[]{:S(2)}) async-start(), calls=%async_computation.1 | async-start | bytes 524288 | tf_op jit(solution)/shard_map/psum | solution.py:14
  7.5 89.4 %copy-start.1 = (bf16[32,64]{1,0:T(8,128)(2,1)S(1)}, bf16[32,64]{1,0:T(8,128)(2,1)}, u32[]{:S(2)}) copy-start(bf16[32,64]{1,0:T(8,128)(2,1)} %param.15) | copy-start | bytes 12292
  9.1 341.1 %reduce-scatter.4.cloned.1.call-start = ((), (), s32[]{:S(2)}) async-start(), calls=%async_computation.2 | async-start | bytes 4259840
Sparse Core Ops, SparseCore 0:
  9.6 82.6 all-reduce.2
  162.9 187.2 reduce-scatter.3
where the time goes:
time: 358 us; the launch traced here: 357 us
  waiting for transfers between devices  265 us (74%)
  other arithmetic  41.2 us (12%)
  local copies, waits for them, and re-layouts  18.3 us (5%)
  loops' own time  13.6 us (4%)
  between operations  13.4 us (4%)
  matrix products  5.32 us (1%)
    unnamed x3, waiting for transfers between devices  187 us
    psum x1, waiting for transfers between devices, spread(): return lax.psum(kept, axis)  77.7 us
    convert_element_type x4, other arithmetic, shards(): (column_virt[None].astype(jnp.float32) * virt_weights[:, None, :]).astype...  21.5 us
    another operation x1, loops' own time, shards(): lax.scan(visit_block, start_terms, jnp.arange(block_count, dtype=jnp.int32))  13.5 us
  transfers between devices with their start and end apart: 2, of which 2 were waited for; matrix products, arithmetic and copies ran while one was open for 2% of the time, Pallas kernels for 0%

commit v1 on v0

--- a/solution.py
+++ b/solution.py
@@ -11,7 +11,7 @@
 
 def spread(value, axis, source):
     kept = jnp.where(lax.axis_index(axis) == source, value, 0).astype(value.dtype)
-    return lax.psum(kept, axis)
+    return jnp.sum(lax.all_gather(kept, axis), axis=0)
 
 
 def quadrature_grids(count_times, count_freqs):

time: 358 us -> 323 us (0.902)
  waiting for transfers between devices: 265 us -> 230 us
    psum x1 -> x0, waiting for transfers between devices: 77.7 us -> none  [spread(): return lax.psum(kept, axis)]
    all_gather x0 -> x1, waiting for transfers between devices: none -> 42.6 us  [spread(): return jnp.sum(lax.all_gather(kept, axis), axis=0)]
where the time goes in v1:
time: 323 us; the launch traced here: 322 us
  waiting for transfers between devices  230 us (71%)
  other arithmetic  41.4 us (13%)
  local copies, waits for them, and re-layouts  18.3 us (6%)
  loops' own time  13.6 us (4%)
  between operations  13.4 us (4%)
  matrix products  5.32 us (2%)
    unnamed x3, waiting for transfers between devices  188 us
    all_gather x1, waiting for transfers between devices, spread(): return jnp.sum(lax.all_gather(kept, axis), axis=0)  42.6 us
    convert_element_type x4, other arithmetic, shards(): (column_virt[None].astype(jnp.float32) * virt_weights[:, None, :]).astype...  21.5 us
    another operation x1, loops' own time, shards(): lax.scan(visit_block, start_terms, jnp.arange(block_count, dtype=jnp.int32))  13.5 us
  transfers between devices with their start and end apart: 2, of which 2 were waited for; matrix products, arithmetic and copies ran while one was open for 2% of the time, Pallas kernels for 0%

profile of v1, /device:TPU:8, one launch (start us, length us, event | category | flops | bytes accessed | tf_op | source)
XLA Modules:
  0.0 322.2 jit_solution(6897014219140031709)
XLA Ops:
  11.8 1.4 multiply_exponential_fusion.1
  13.2 1.5 multiply_exponential_fusion
  14.6 42.6 %all-gather.2.cloned.1.call-done = bf16[8,64,2048]{2,1,0:T(8,128)(2,1)} async-done(((bf16[1,64,2048]{2,1,0:T(8,128)(2,1)}), bf16[8,64,2048]{2,1,0:T(8,128)(2,1)}) %all-gather.2.cloned.1.call-update) | async-done | bytes 2097168 | tf_op jit(solution)/shard_map/all_gather | solution.py:14
  57.2 2.0 reduce_sum.12
  60.4 1.6 broadcast_in_dim.7.clone
  62.0 56.1 %while.11 = (s32[]{:T(128)}, f32[32,32,512]{2,0,1:T(8,128)}, s32[4]{0:T(128)}, pred[4,64]{1,0:T(4,128)(4,1)}, bf16[512,512]{1,0:T(8,128)(2,1)}, /*index=5*/bf16[...) while((s32[]{:T(128)}, f32[32,32,512]{2,0,1:T(8,128)}, ...), condition=%wide.region_6.7_spmd.clone, body=%wide.region_2.6_spmd.clone.sunk | while | flops 1099694208 | bytes 21763300 | solution.py:94
  62.0 1.3 dynamic_slice.49
  65.3 1.3 dynamic-slice_reduce_fusion.2
  67.2 5.4 %multiply_convert_fusion.5 = bf16[32,64,1536]{2,1,0:T(8,128)(2,1)} fusion(f32[32,1536]{1,0:T(8,128)} %get-tuple-element.256, f32[64,1536]{1,0:T(8,128)S(1)} %get-tuple-element.257), kind=kLoop, calls=%fused_computation.19.clone.1 | loop fusion | flops 6291456 | bytes 6881280 | tf_op jit(solution)/shard_map/convert_element_type | solution.py:60
  72.5 1.5 multiply_convert_fusion.4
  76.0 1.3 dynamic_slice.49
  81.2 5.4 %multiply_convert_fusion.5 = bf16[32,64,1536]{2,1,0:T(8,128)(2,1)} fusion(f32[32,1536]{1,0:T(8,128)} %get-tuple-element.256, f32[64,1536]{1,0:T(8,128)S(1)} %get-tuple-element.257), kind=kLoop, calls=%fused_computation.19.clone.1 | loop fusion | flops 6291456 | bytes 6881280 | tf_op jit(solution)/shard_map/convert_element_type | solution.py:60
  86.6 1.5 multiply_convert_fusion.4
  90.1 1.3 dynamic_slice.49
  93.4 1.3 dynamic-slice_reduce_fusion.2
  95.2 5.4 %multiply_convert_fusion.5 = bf16[32,64,1536]{2,1,0:T(8,128)(2,1)} fusion(f32[32,1536]{1,0:T(8,128)} %get-tuple-element.256, f32[64,1536]{1,0:T(8,128)S(1)} %get-tuple-element.257), kind=kLoop, calls=%fused_computation.19.clone.1 | loop fusion | flops 6291456 | bytes 6881280 | tf_op jit(solution)/shard_map/convert_element_type | solution.py:60
  100.6 1.5 multiply_convert_fusion.4
  104.1 1.3 dynamic_slice.49
  107.4 1.3 dynamic-slice_reduce_fusion.2
  109.2 5.4 %multiply_convert_fusion.5 = bf16[32,64,1536]{2,1,0:T(8,128)(2,1)} fusion(f32[32,1536]{1,0:T(8,128)} %get-tuple-element.256, f32[64,1536]{1,0:T(8,128)S(1)} %get-tuple-element.257), kind=kLoop, calls=%fused_computation.19.clone.1 | loop fusion | flops 6291456 | bytes 6881280 | tf_op jit(solution)/shard_map/convert_element_type | solution.py:60
  114.6 1.5 multiply_convert_fusion.4
  118.1 5.3 %fusion.22 = f32[64,32,512]{2,0,1:T(8,128)S(1)} fusion(f32[32,32,512]{2,0,1:T(8,128)} %get-tuple-element.81, f32[32]{0:T(128)} %get-tuple-element.137, f32[64]{0:T(128)} %add_exponential_fusion, f32[32]{0:T(128)} %get-tuple-element.138), kind=kOutput, calls=%fused_computation.30 | convolution fusion | flops 402657280 | bytes 6291968 | tf_op jit(solution)/shard_map/kt,tvr->kvr/dot_general | solution.py:96
  123.5 4.4 %copy.15 = f32[64,32,512]{2,1,0:T(8,128)} copy(f32[64,32,512]{2,0,1:T(8,128)S(1)} %fusion.22) | data formatting | bytes 8388608 | tf_op jit(solution)/shard_map/kt,tvr->kvr/dot_general | solution.py:96
  127.8 187.5 %reduce-scatter.4.cloned.1.call-done = f32[1,32,512]{2,1,0:T(8,128)} async-done(((f32[64,32,512]{2,1,0:T(8,128)}), f32[1,32,512]{2,1,0:T(8,128)}) %reduce-scatter.4.cloned.1.call-update) | async-done | bytes 65552
  (35 shorter events, 12.8 us)
Async XLA Ops:
  6.5 2.7 copy-start
  6.5 50.7 %all-gather.2.cloned.1.call-start = ((), (), s32[]{:S(2)}) async-start(), calls=%async_computation.1 | async-start | bytes 2359296 | tf_op jit(solution)/shard_map/all_gather | solution.py:14
  9.2 306.2 %reduce-scatter.4.cloned.1.call-start = ((), (), s32[]{:S(2)}) async-start(), calls=%async_computation.2 | async-start | bytes 4259840
  14.6 47.3 %copy-start.1 = (bf16[32,64]{1,0:T(8,128)(2,1)S(1)}, bf16[32,64]{1,0:T(8,128)(2,1)}, u32[]{:S(2)}) copy-start(bf16[32,64]{1,0:T(8,128)(2,1)} %param.15) | copy-start | bytes 12292
Sparse Core Ops, SparseCore 0:
  9.4 47.7 all-gather.1
  128.0 187.3 reduce-scatter.3
